TPU v7x, 32 devices: a whole 2x2x4 slice. The times are simulated.
32 devices in a mesh: rep: 4 (over y, core), dp: 8 (over z, x).
Axes of the slice: x: 2, y: 2, z: 4, core: 2. Of those that a mesh axis runs over, the one named last changes fastest.
Arguments:
- query_states: bfloat16 [256, 32, 768], P(('rep', 'dp')), may hold values from -12 to 12
- passage_states: bfloat16 [128, 180, 768], P(('rep', 'dp')), may hold values from -12 to 12
- query_lengths: int32 [256], P(('rep', 'dp')), may hold values from 8 to 32, as said below
- passage_lengths: int32 [128], P(('rep', 'dp')), may hold values from 45 to 180, as said below
- passage_ids: int32 [128, 180], P(('rep', 'dp')), may hold values from 2 to 30521, as said below
- positives: int32 [256], P(('rep', 'dp')), may hold values from 0 to 31, as said below
- up_weight: bfloat16 [768, 3072], replicated, may hold values from -0.21875 to 0.21875
- up_bias: float32 [3072], replicated, may hold values from -3 to 3
- down_weight: bfloat16 [3072, 768], replicated, may hold values from -0.109375 to 0.109375
- down_bias: float32 [768], replicated, may hold values from -3 to 3
- norm_gain: float32 [768], replicated, may hold values from 0.5 to 1.5
- norm_bias: float32 [768], replicated, may hold values from -2 to 2
- proj_weight: bfloat16 [768, 128], replicated, may hold values from -0.21875 to 0.21875
Outputs:
- mean_loss: float32 [], replicated
- passage_grad: float32 [128, 180, 128], P(('rep', 'dp'))
- proj_grad: float32 [768, 128], replicated
Inputs may be any that keep to these rules, and one draw needn't show every extreme that they name: `query_lengths`: every device holds a query with all 32 slots real. `passage_lengths`: every device holds a passage with all 180 slots real. `passage_ids`: slots 0 and 1 of every passage hold ids 101 and 2; ids 999 to 1066 are punctuation. `positives`: index of the positive passage among the 32 passages of the query's replica group, in the order of the devices.
All inputs are finite; a program needn't handle non-finite values.
Results may differ from a plain program's by a relative error of at most 0.0055.
Values may be sent and summed in bfloat16 or wider, within the bound.
A program may use at most 128 MiB of HBM per device.

v0:
```python
import math
import jax
import jax.numpy as jnp
from jax import lax
from jax.sharding import PartitionSpec as P

temper = 0.05
eps_norm = 1e-06
punct_low = 999
punct_high = 1067


def encode_rows(
    token_rows, up_weight, up_bias, down_weight, down_bias, norm_gain, norm_bias, proj_weight
):
    upward = jnp.dot(token_rows, up_weight, preferred_element_type=jnp.float32) + up_bias
    activated = jax.nn.gelu(upward, approximate=False).astype(jnp.bfloat16)
    residual = (
        token_rows.astype(jnp.float32)
        + jnp.dot(activated, down_weight, preferred_element_type=jnp.float32)
        + down_bias
    )
    average = jnp.mean(residual, -1, keepdims=True)
    centered = residual - average
    variance = jnp.mean(centered * centered, -1, keepdims=True)
    hidden = (centered * lax.rsqrt(variance + eps_norm) * norm_gain + norm_bias).astype(
        jnp.bfloat16
    )
    projected = jnp.dot(hidden, proj_weight, preferred_element_type=jnp.float32)
    inverse = lax.rsqrt(jnp.sum(projected * projected, -1, keepdims=True) + eps_norm)
    return (hidden, projected * inverse, inverse)


def token_scores(query_flat, query_keep, block_emb, block_keep, query_count):
    item_count, pass_len, embed_dim = block_emb.shape
    flat_block = block_emb.reshape(item_count * pass_len, embed_dim)
    similar = lax.dot_general(
        query_flat, flat_block, (((1,), (1,)), ((), ())), preferred_element_type=jnp.float32
    )
    weights = (
        jnp.exp(similar / temper).reshape(-1, item_count, pass_len)
        * block_keep.astype(jnp.float32)[None]
    )
    totals = jnp.sum(weights, -1)
    soft_max = temper * jnp.log(totals) * query_keep[:, None]
    scores = jnp.sum(soft_max.reshape(query_count, -1, item_count), 1)
    return (scores, weights, totals)


def token_grads(query_flat, query_keep, block_emb, weights, totals, dscore, query_count):
    item_count, pass_len, embed_dim = block_emb.shape
    factor = (dscore[:, None, :] * query_keep.reshape(query_count, -1)[:, :, None]).reshape(
        -1, item_count
    ) / totals
    sim_grad = (
        (weights * factor[:, :, None]).reshape(-1, item_count * pass_len).astype(jnp.bfloat16)
    )
    flat_block = block_emb.reshape(item_count * pass_len, embed_dim)
    passage_term = lax.dot_general(
        sim_grad, query_flat, (((0,), (0,)), ((), ())), preferred_element_type=jnp.float32
    )
    query_term = jnp.dot(sim_grad, flat_block, preferred_element_type=jnp.float32)
    return (passage_term.reshape(item_count, pass_len, embed_dim), query_term)


def cross_entropy(scores, positives):
    log_total = jnp.log(jnp.sum(jnp.exp(scores), 1))
    onehot = (jnp.arange(scores.shape[1], dtype=jnp.int32)[None, :] == positives[:, None]).astype(
        jnp.float32
    )
    loss_sum = jnp.sum(log_total - jnp.sum(scores * onehot, 1))
    dscore = jnp.exp(scores - log_total[:, None]) - onehot
    return (loss_sum, dscore)


def norm_backward(gradient, normed, inverse):
    return (inverse * (gradient - normed * jnp.sum(normed * gradient, -1, keepdims=True))).astype(
        jnp.bfloat16
    )


def per_device(
    query_states,
    passage_states,
    query_lengths,
    passage_lengths,
    passage_ids,
    positives,
    up_weight,
    up_bias,
    down_weight,
    down_bias,
    norm_gain,
    norm_bias,
    proj_weight,
):
    query_count, query_len, model_width = query_states.shape
    pass_count, pass_len, _ = passage_states.shape
    embed_dim = proj_weight.shape[1]
    token_rows = jnp.concatenate(
        [query_states.reshape(-1, model_width), passage_states.reshape(-1, model_width)], 0
    )
    hidden, normed, inverse = encode_rows(
        token_rows, up_weight, up_bias, down_weight, down_bias, norm_gain, norm_bias, proj_weight
    )
    boundary = query_count * query_len
    query_emb = normed[:boundary].astype(jnp.bfloat16)
    pass_emb = normed[boundary:].astype(jnp.bfloat16).reshape(pass_count, pass_len, embed_dim)
    query_keep = (
        (jnp.arange(query_len, dtype=jnp.int32)[None, :] < query_lengths[:, None])
        .astype(jnp.float32)
        .reshape(-1)
    )
    is_punct = (passage_ids >= punct_low) & (passage_ids < punct_high)
    pass_keep = (
        (jnp.arange(pass_len, dtype=jnp.int32)[None, :] < passage_lengths[:, None])
        & jnp.logical_not(is_punct)
    ).astype(jnp.bfloat16)
    groups = lax.axis_size("dp")
    gathered, gathered_keep = (
        lax.all_gather(pass_emb, "dp", axis=0, tiled=True),
        lax.all_gather(pass_keep, "dp", axis=0, tiled=True),
    )
    group_pass = pass_count * groups
    block_pass = math.gcd(group_pass, 16)
    block_count = group_pass // block_pass
    emb_blocks = gathered.reshape(block_count, block_pass, pass_len, embed_dim)
    keep_blocks = gathered_keep.reshape(block_count, block_pass, pass_len)

    def forward(paired):
        scores, _, _ = token_scores(query_emb, query_keep, paired[0], paired[1], query_count)
        return scores

    stacked = lax.map(forward, (emb_blocks, keep_blocks))
    scores = jnp.transpose(stacked, (1, 0, 2)).reshape(query_count, group_pass)
    loss_sum, dscore = cross_entropy(scores, positives)
    grad_blocks = jnp.transpose(dscore.reshape(query_count, block_count, block_pass), (1, 0, 2))

    def backward(query_grad, triple):
        block_emb, block_keep, block_grad = triple
        _, weights, totals = token_scores(query_emb, query_keep, block_emb, block_keep, query_count)
        passage_term, query_term = token_grads(
            query_emb, query_keep, block_emb, weights, totals, block_grad, query_count
        )
        return (query_grad + query_term, passage_term)

    start_grad = jnp.zeros((query_count * query_len, embed_dim), jnp.float32)
    query_grad, pass_terms = lax.scan(backward, start_grad, (emb_blocks, keep_blocks, grad_blocks))
    passage_grad = lax.psum_scatter(
        pass_terms.reshape(group_pass, pass_len, embed_dim), "dp", scatter_dimension=0, tiled=True
    )
    query_back = norm_backward(query_grad, normed[:boundary], inverse[:boundary])
    pass_back = norm_backward(
        passage_grad.reshape(-1, embed_dim), normed[boundary:], inverse[boundary:]
    )
    all_back = jnp.concatenate([query_back, pass_back], 0)
    local_sum = lax.dot_general(
        hidden, all_back, (((0,), (0,)), ((), ())), preferred_element_type=jnp.float32
    )
    proj_total, loss_total = lax.psum((local_sum, loss_sum), ("rep", "dp"))
    mean_loss = loss_total / (query_count * lax.axis_size("rep") * groups)
    return (mean_loss, passage_grad, proj_total)


def solution(mesh):
    in_specs = (
        P(("rep", "dp"), None, None),
        P(("rep", "dp"), None, None),
        P(("rep", "dp")),
        P(("rep", "dp")),
        P(("rep", "dp"), None),
        P(("rep", "dp")),
        P(),
        P(),
        P(),
        P(),
        P(),
        P(),
        P(),
    )
    out_specs = (P(), P(("rep", "dp"), None, None), P())
    return jax.shard_map(
        per_device, mesh=mesh, in_specs=in_specs, out_specs=out_specs, check_vma=False
    )
```

profile of v0, /device:TPU:0, one launch (start us, length us, event | category | flops | bytes accessed | tf_op | source)
XLA Modules:
  0.0 375.2 jit_solution(12768285296816217812)
XLA Ops:
  9.8 39.0 %fusion.77 = (f32[976]{0:T(1024)S(1)}, f32[976,768]{1,0:T(8,128)S(1)}) fusion(f32[768]{0:T(1024)} %param.26, bf16[3072,768]{1,0:T(8,128)(2,1)} %param.25, f32[3072]{0:T(1024)} %param.24, bf16[768,3072]{1,0:T(8,128)(2,1)} %param.23, bf16[720,768]{1,0:T(8,128)(2,1)} %reshape.166, bf16[256,768]{1,0:T(8,128)(2,1)} %bitcast.86), kind=kOutput, calls=%fused_computation.113 | convolution fusion | flops 9416821760 | bytes 13953856 | tf_op jit(solution)/shard_map/dot_general | solution.py:20
  53.0 27.9 %all-gather = bf16[8,4,180]{2,1,0:T(4,128)(2,1)S(1)} all-gather(bf16[1,4,180]{2,1,0:T(4,128)(2,1)S(1)} %fusion.42), channel_id=1, replica_groups=mesh['rep'=4,'dp'=8] {'dp'}, dimensions={0}, use_global_device_ids=true | all-gather | bytes 12960 | tf_op jit(solution)/shard_map/all_gather | solution.py:122
  80.9 18.3 %all-gather.3.cloned.1.call-done = bf16[32,180,128]{2,1,0:T(8,128)(2,1)} async-done(((bf16[4,180,128]{2,1,0:T(8,128)(2,1)}), bf16[32,180,128]{2,1,0:T(8,128)(2,1)}) %all-gather.3.cloned.1.call-update) | async-done | bytes 1474576 | tf_op jit(solution)/shard_map/all_gather | solution.py:121
  99.3 13.9 %while.24 = (s32[]{:T(128)}, f32[2,8,16]{2,1,0:T(8,128)S(1)}, bf16[2,16,180,128]{3,2,1,0:T(8,128)(2,1)}, bf16[256,128]{1,0:T(8,128)(2,1)S(1)}, bf16[2,16,180]{2,1,0:T(8,128)(2,1)S(1)}, /*index=5*/s32[8]{0:T(128)S(1)}, s32[]{:T(128)}) while((s32[]{:T(128)}, f32[2,8,16]{2,1,0:T(8,128)S(1)}, bf16[2,16,180,128]{3,2,1,0:T(8,128)(2,1)}, ...), condition=%wide.region_6.7_spmd.clone, body=%wide.region_3.6_spmd.clone.sunk | while | flops 190962880 | bytes 15687425 | solution.py:134
  100.7 2.2 fusion.106
  102.9 2.6 reshape.189
  107.6 2.2 fusion.106
  109.8 2.6 reshape.189
  114.1 45.3 %while.25 = (s32[]{:T(128)}, f32[256,128]{1,0:T(8,128)S(1)}, f32[2,16,180,128]{3,2,1,0:T(8,128)}, bf16[2,16,180,128]{3,2,1,0:T(8,128)(2,1)}, bf16[256,128]{1,0:T...) while((s32[]{:T(128)}, f32[256,128]{1,0:T(8,128)S(1)}, ...), condition=%wide.region_13.14_spmd.clone, body=%wide.region_11.13_spmd.clone.sunk | while | flops 570727744 | bytes 49299292 | solution.py:148
  118.5 1.8 reshape.191
  120.3 2.3 multiply_reduce_fusion.12
  122.7 1.9 mul.316
  124.5 4.1 %mul.317 = f32[256,2880]{0,1:T(8,128)} reshape(f32[256,16,180]{0,2,1:T(8,128)} %mul.316) | data formatting | bytes 5898240 | tf_op jit(solution)/shard_map/while/body/eval_jaxpr/mul | solution.py:56
  128.7 2.3 multiply_convert_fusion.4
  132.8 2.3 reshape.192
  141.2 1.8 reshape.191
  143.0 2.3 multiply_reduce_fusion.12
  145.3 1.9 mul.316
  147.2 4.1 %mul.317 = f32[256,2880]{0,1:T(8,128)} reshape(f32[256,16,180]{0,2,1:T(8,128)} %mul.316) | data formatting | bytes 5898240 | tf_op jit(solution)/shard_map/while/body/eval_jaxpr/mul | solution.py:56
  151.3 2.3 multiply_convert_fusion.4
  155.5 2.3 reshape.192
  161.7 70.0 %reduce-scatter.2.cloned.1.call-done = f32[4,180,128]{2,1,0:T(8,128)} async-done(((f32[32,180,128]{2,1,0:T(8,128)}), f32[4,180,128]{2,1,0:T(8,128)}) %reduce-scatter.2.cloned.1.call-update) | async-done | bytes 368656 | tf_op jit(solution)/shard_map/reduce_scatter | solution.py:149
  235.6 39.9 %psum.14 = f32[]{:T(128)} all-reduce(f32[]{:T(128)} %get-tuple-element.165), channel_id=1, replica_groups=mesh['rep'=4,'dp'=8] {'rep','dp'}, use_global_device_ids=true, to_apply=%region_10.11 | all-reduce | flops 1 | bytes 8 | tf_op jit(solution)/shard_map/psum | solution.py:160
  277.0 88.8 %all-reduce.2.cloned.1.call-done = f32[768,128]{1,0:T(8,128)} async-done(((f32[768,128]{1,0:T(8,128)}), f32[768,128]{1,0:T(8,128)}) %all-reduce.2.cloned.1.call-update) | async-done | bytes 393232 | tf_op jit(solution)/shard_map/psum | solution.py:160
  (117 shorter events, 36.1 us)
Async XLA Ops:
  7.2 43.8 %copy-start = (bf16[768,128]{1,0:T(8,128)(2,1)S(1)}, bf16[768,128]{1,0:T(8,128)(2,1)}, u32[]{:S(2)}) copy-start(bf16[768,128]{1,0:T(8,128)(2,1)} %param.29) | copy-start | bytes 589828
  7.2 92.1 %all-gather.3.cloned.1.call-start = ((), (), s32[]{:S(2)}) async-start(), calls=%async_computation.1 | async-start | bytes 1695744 | tf_op jit(solution)/shard_map/all_gather | solution.py:121
  9.7 39.6 %copy-start.10 = (f32[768]{0:T(1024)S(1)}, f32[768]{0:T(1024)}, u32[]{:S(2)}) copy-start(f32[768]{0:T(1024)} %param.28) | copy-start | bytes 9220
  9.8 39.6 %copy-start.11 = (f32[768]{0:T(1024)S(1)}, f32[768]{0:T(1024)}, u32[]{:S(2)}) copy-start(f32[768]{0:T(1024)} %param.27) | copy-start | bytes 9220
  49.3 3.6 copy-start.9
  49.3 3.6 copy-start.13
  49.3 50.0 %copy-start.8 = (s32[8]{0:T(128)S(1)}, s32[8]{0:T(128)}, u32[]{:S(2)}) copy-start(s32[8]{0:T(128)} %param.19) | copy-start | bytes 100
  49.9 1.1 copy-start.3
  51.9 47.4 %copy-start.5 = (f32[976,128]{1,0:T(8,128)}, f32[976,128]{1,0:T(8,128)S(1)}, u32[]{:S(2)}) copy-start(f32[976,128]{1,0:T(8,128)S(1)} %broadcast_multiply_fusion) | copy-start | bytes 1499140
  52.8 178.9 %reduce-scatter.2.cloned.1.call-start = ((), (), s32[]{:S(2)}) async-start(), calls=%async_computation.2 | async-start | bytes 3391488 | tf_op jit(solution)/shard_map/reduce_scatter | solution.py:149
  99.3 13.9 %copy-start.12 = (s32[8]{0:T(128)S(1)}, s32[8]{0:T(128)}, u32[]{:S(2)}) copy-start(s32[8]{0:T(128)} %param.22) | copy-start | bytes 100
  128.7 3.5 copy-start.2
  131.0 1.1 copy-start.1
  151.3 3.5 copy-start.2
  153.7 1.1 copy-start.1
  159.4 74.5 %copy-start.6 = (f32[976,128]{1,0:T(8,128)S(1)}, f32[976,128]{1,0:T(8,128)}, u32[]{:S(2)}) copy-start(f32[976,128]{1,0:T(8,128)} %copy-done.5) | copy-start | bytes 1499140
  159.4 74.8 %copy-start.4 = (bf16[976,768]{1,0:T(8,128)(2,1)S(1)}, bf16[976,768]{1,0:T(8,128)(2,1)}, u32[]{:S(2)}) copy-start(bf16[976,768]{1,0:T(8,128)(2,1)} %copy-done.3) | copy-start | bytes 4497412
  159.4 206.4 %all-reduce.2.cloned.1.call-start = ((), (), s32[]{:S(2)}) async-start(), calls=%async_computation.3 | async-start | bytes 786432 | tf_op jit(solution)/shard_map/psum | solution.py:160
  231.7 44.5 %copy-start.7 = (f32[4,180,128]{2,1,0:T(8,128)S(1)}, f32[4,180,128]{2,1,0:T(8,128)}, u32[]{:S(2)}) copy-start(f32[4,180,128]{2,1,0:T(8,128)} %reduce-scatter.2.cloned.1.call-done) | copy-start | bytes 1105924
Sparse Core Ops, SparseCore 0:
  52.9 46.3 all-gather.2
  159.6 72.0 reduce-scatter.1
  237.6 128.1 all-reduce.1
where the time goes:
time: 376 us; the launch traced here: 375 us
  waiting for transfers between devices  177 us (47%)
  blocking collectives  67.8 us (18%)
  matrix products  53.4 us (14%)
  local copies, waits for them, and re-layouts  44.1 us (12%)
  other arithmetic  16.6 us (4%)
  between operations  15.8 us (4%)
    psum x1, waiting for transfers between devices, per_device(): proj_total, loss_total = lax.psum((local_sum, loss_sum), ('rep', 'dp'))  88.8 us
    reduce_scatter x1, waiting for transfers between devices, per_device(): lax.psum_scatter(pass_terms.reshape(group_pass, pass_len, embed_dim), 'dp...  70 us
    psum x1, blocking collectives, per_device(): proj_total, loss_total = lax.psum((local_sum, loss_sum), ('rep', 'dp'))  39.9 us
    dot_general x1, matrix products, encode_rows(): jnp.dot(activated, down_weight, preferred_element_type=jnp.float32)  39 us
    all_gather x1, blocking collectives, per_device(): lax.all_gather(pass_keep, 'dp', axis=0, tiled=True)  27.9 us
    all_gather x1, waiting for transfers between devices, per_device(): lax.all_gather(pass_emb, 'dp', axis=0, tiled=True)  18.3 us
    mul x4, local copies, waits for them, and re-layouts, token_grads(): weights * factor[:, :, None]  12 us
    reshape x4, local copies, waits for them, and re-layouts, token_scores(): jnp.exp(similar / temper).reshape(-1, item_count, pass_len)  8.91 us
  transfers between devices with their start and end apart: 3, of which 3 were waited for; matrix products, arithmetic and copies ran while one was open for 1% of the time, Pallas kernels for 0%

commit v1 on v0

--- a/solution.py
+++ b/solution.py
@@ -94,6 +94,10 @@
     norm_bias,
     proj_weight,
 ):
+
+    def reach_cells(shard_axis, axis_tag, a0):
+        return jax.lax.psum(jax.lax.psum(a0, shard_axis), axis_tag)
+
     query_count, query_len, model_width = query_states.shape
     pass_count, pass_len, _ = passage_states.shape
     embed_dim = proj_weight.shape[1]
@@ -157,7 +161,7 @@
     local_sum = lax.dot_general(
         hidden, all_back, (((0,), (0,)), ((), ())), preferred_element_type=jnp.float32
     )
-    proj_total, loss_total = lax.psum((local_sum, loss_sum), ("rep", "dp"))
+    proj_total, loss_total = reach_cells("dp", "rep", (local_sum, loss_sum))
     mean_loss = loss_total / (query_count * lax.axis_size("rep") * groups)
     return (mean_loss, passage_grad, proj_total)
 

time: 376 us -> 351 us (0.934)
  blocking collectives: 67.8 us -> 54.3 us
  waiting for transfers between devices: 177 us -> 166 us
    psum x1 -> x2, blocking collectives: 39.9 us -> 26.3 us  [reach_cells(): return jax.lax.psum(jax.lax.psum(a0, shard_axis), axis_tag)]
    psum x1 -> x2, waiting for transfers between devices: 88.8 us -> 77.4 us  [reach_cells(): return jax.lax.psum(jax.lax.psum(a0, shard_axis), axis_tag)]
  transfers between devices with their start and end apart: 3 -> 4, of which waited for: 3 -> 4; matrix products, arithmetic and copies ran while one was open for 1% -> 1% of each run, Pallas kernels for 0% -> 0%
where the time goes in v1:
time: 351 us; the launch traced here: 350 us
  waiting for transfers between devices  166 us (47%)
  blocking collectives  54.3 us (15%)
  matrix products  53.4 us (15%)
  local copies, waits for them, and re-layouts  44.1 us (13%)
  other arithmetic  16.6 us (5%)
  between operations  15.8 us (5%)
    psum x2, waiting for transfers between devices, reach_cells(): return jax.lax.psum(jax.lax.psum(a0, shard_axis), axis_tag)  77.4 us
    reduce_scatter x1, waiting for transfers between devices, per_device(): lax.psum_scatter(pass_terms.reshape(group_pass, pass_len, embed_dim), 'dp...  70 us
    dot_general x1, matrix products, encode_rows(): jnp.dot(activated, down_weight, preferred_element_type=jnp.float32)  39 us
    all_gather x1, blocking collectives, per_device(): lax.all_gather(pass_keep, 'dp', axis=0, tiled=True)  27.9 us
    psum x2, blocking collectives, reach_cells(): return jax.lax.psum(jax.lax.psum(a0, shard_axis), axis_tag)  26.3 us
    all_gather x1, waiting for transfers between devices, per_device(): lax.all_gather(pass_emb, 'dp', axis=0, tiled=True)  18.3 us
    mul x4, local copies, waits for them, and re-layouts, token_grads(): weights * factor[:, :, None]  12 us
    reshape x4, local copies, waits for them, and re-layouts, token_scores(): jnp.exp(similar / temper).reshape(-1, item_count, pass_len)  8.91 us
  transfers between devices with their start and end apart: 4, of which 4 were waited for; matrix products, arithmetic and copies ran while one was open for 1% of the time, Pallas kernels for 0%

profile of v1, /device:TPU:0, one launch (start us, length us, event | category | flops | bytes accessed | tf_op | source)
XLA Modules:
  0.0 350.3 jit_solution(7419014983253992372)
XLA Ops:
  9.8 39.0 %fusion.77 = (f32[976]{0:T(1024)S(1)}, f32[976,768]{1,0:T(8,128)S(1)}) fusion(f32[768]{0:T(1024)} %param.26, bf16[3072,768]{1,0:T(8,128)(2,1)} %param.25, f32[3072]{0:T(1024)} %param.24, bf16[768,3072]{1,0:T(8,128)(2,1)} %param.23, bf16[720,768]{1,0:T(8,128)(2,1)} %reshape.166, bf16[256,768]{1,0:T(8,128)(2,1)} %bitcast.86), kind=kOutput, calls=%fused_computation.113 | convolution fusion | flops 9416821760 | bytes 13953856 | tf_op jit(solution)/shard_map/dot_general | solution.py:20
  53.0 27.9 %all-gather = bf16[8,4,180]{2,1,0:T(4,128)(2,1)S(1)} all-gather(bf16[1,4,180]{2,1,0:T(4,128)(2,1)S(1)} %fusion.42), channel_id=1, replica_groups=mesh['rep'=4,'dp'=8] {'dp'}, dimensions={0}, use_global_device_ids=true | all-gather | bytes 12960 | tf_op jit(solution)/shard_map/all_gather | solution.py:126
  80.9 18.3 %all-gather.3.cloned.1.call-done = bf16[32,180,128]{2,1,0:T(8,128)(2,1)} async-done(((bf16[4,180,128]{2,1,0:T(8,128)(2,1)}), bf16[32,180,128]{2,1,0:T(8,128)(2,1)}) %all-gather.3.cloned.1.call-update) | async-done | bytes 1474576 | tf_op jit(solution)/shard_map/all_gather | solution.py:125
  99.3 13.9 %while.24 = (s32[]{:T(128)}, f32[2,8,16]{2,1,0:T(8,128)S(1)}, bf16[2,16,180,128]{3,2,1,0:T(8,128)(2,1)}, bf16[256,128]{1,0:T(8,128)(2,1)S(1)}, bf16[2,16,180]{2,1,0:T(8,128)(2,1)S(1)}, /*index=5*/s32[8]{0:T(128)S(1)}, s32[]{:T(128)}) while((s32[]{:T(128)}, f32[2,8,16]{2,1,0:T(8,128)S(1)}, bf16[2,16,180,128]{3,2,1,0:T(8,128)(2,1)}, ...), condition=%wide.region_6.7_spmd.clone, body=%wide.region_3.6_spmd.clone.sunk | while | flops 190962880 | bytes 15687425 | solution.py:138
  100.7 2.2 fusion.106
  102.9 2.6 reshape.189
  107.6 2.2 fusion.106
  109.8 2.6 reshape.189
  114.1 45.3 %while.25 = (s32[]{:T(128)}, f32[256,128]{1,0:T(8,128)S(1)}, f32[2,16,180,128]{3,2,1,0:T(8,128)}, bf16[2,16,180,128]{3,2,1,0:T(8,128)(2,1)}, bf16[256,128]{1,0:T...) while((s32[]{:T(128)}, f32[256,128]{1,0:T(8,128)S(1)}, ...), condition=%wide.region_14.15_spmd.clone, body=%wide.region_12.14_spmd.clone.sunk | while | flops 570727744 | bytes 49299292 | solution.py:152
  120.3 2.3 multiply_reduce_fusion.12
  122.7 1.9 mul.316
  124.5 4.1 %mul.317 = f32[256,2880]{0,1:T(8,128)} reshape(f32[256,16,180]{0,2,1:T(8,128)} %mul.316) | data formatting | bytes 5898240 | tf_op jit(solution)/shard_map/while/body/eval_jaxpr/mul | solution.py:56
  128.7 2.3 multiply_convert_fusion.4
  132.8 2.3 reshape.192
  143.0 2.3 multiply_reduce_fusion.12
  145.3 1.9 mul.316
  147.2 4.1 %mul.317 = f32[256,2880]{0,1:T(8,128)} reshape(f32[256,16,180]{0,2,1:T(8,128)} %mul.316) | data formatting | bytes 5898240 | tf_op jit(solution)/shard_map/while/body/eval_jaxpr/mul | solution.py:56
  151.3 2.3 multiply_convert_fusion.4
  155.5 2.3 reshape.192
  161.7 70.0 %reduce-scatter.2.cloned.1.call-done = f32[4,180,128]{2,1,0:T(8,128)} async-done(((f32[32,180,128]{2,1,0:T(8,128)}), f32[4,180,128]{2,1,0:T(8,128)}) %reduce-scatter.2.cloned.1.call-update) | async-done | bytes 368656 | tf_op jit(solution)/shard_map/reduce_scatter | solution.py:153
  235.7 71.2 %all-reduce.3.cloned.1.call-done = f32[768,128]{1,0:T(8,128)} async-done(((f32[768,128]{1,0:T(8,128)}), f32[768,128]{1,0:T(8,128)}) %all-reduce.3.cloned.1.call-update) | async-done | bytes 393232 | tf_op jit(solution)/shard_map/psum | solution.py:99
  306.8 20.1 %psum.28 = f32[]{:T(128)} all-reduce(f32[]{:T(128)} %get-tuple-element.165), channel_id=1, replica_groups=mesh['rep'=4,'dp'=8] {'dp'}, use_global_device_ids=true, to_apply=%region_10.11 | all-reduce | flops 1 | bytes 8 | tf_op jit(solution)/shard_map/psum | solution.py:99
  326.9 6.3 %psum.29 = f32[]{:T(128)} all-reduce(f32[]{:T(128)} %psum.28), channel_id=1, replica_groups=mesh['rep'=4,'dp'=8] {'rep'}, use_global_device_ids=true, to_apply=%region_11.12 | all-reduce | flops 1 | bytes 8 | tf_op jit(solution)/shard_map/psum | solution.py:99
  334.7 6.3 %all-reduce.5.cloned.1.call-done = f32[768,128]{1,0:T(8,128)} async-done(((f32[768,128]{1,0:T(8,128)}), f32[768,128]{1,0:T(8,128)}) %all-reduce.5.cloned.1.call-update) | async-done | bytes 393232 | tf_op jit(solution)/shard_map/psum | solution.py:99
  (121 shorter events, 39.8 us)
Async XLA Ops:
  7.2 43.8 %copy-start = (bf16[768,128]{1,0:T(8,128)(2,1)S(1)}, bf16[768,128]{1,0:T(8,128)(2,1)}, u32[]{:S(2)}) copy-start(bf16[768,128]{1,0:T(8,128)(2,1)} %param.29) | copy-start | bytes 589828
  7.2 92.1 %all-gather.3.cloned.1.call-start = ((), (), s32[]{:S(2)}) async-start(), calls=%async_computation.1 | async-start | bytes 1695744 | tf_op jit(solution)/shard_map/all_gather | solution.py:125
  9.7 39.6 %copy-start.10 = (f32[768]{0:T(1024)S(1)}, f32[768]{0:T(1024)}, u32[]{:S(2)}) copy-start(f32[768]{0:T(1024)} %param.28) | copy-start | bytes 9220
  9.8 39.6 %copy-start.11 = (f32[768]{0:T(1024)S(1)}, f32[768]{0:T(1024)}, u32[]{:S(2)}) copy-start(f32[768]{0:T(1024)} %param.27) | copy-start | bytes 9220
  49.3 3.6 %copy-start.9 = (s32[4,180]{1,0:T(4,128)S(1)}, s32[4,180]{1,0:T(4,128)}, u32[]{:S(2)}) copy-start(s32[4,180]{1,0:T(4,128)} %param.21) | copy-start | bytes 8644
  49.3 3.6 %copy-start.13 = (s32[4]{0:T(128)S(1)}, s32[4]{0:T(128)}, u32[]{:S(2)}) copy-start(s32[4]{0:T(128)} %param.20) | copy-start | bytes 52
  49.3 50.0 %copy-start.8 = (s32[8]{0:T(128)S(1)}, s32[8]{0:T(128)}, u32[]{:S(2)}) copy-start(s32[8]{0:T(128)} %param.19) | copy-start | bytes 100
  49.9 1.1 copy-start.3
  51.9 47.4 %copy-start.5 = (f32[976,128]{1,0:T(8,128)}, f32[976,128]{1,0:T(8,128)S(1)}, u32[]{:S(2)}) copy-start(f32[976,128]{1,0:T(8,128)S(1)} %broadcast_multiply_fusion) | copy-start | bytes 1499140
  52.8 178.9 %reduce-scatter.2.cloned.1.call-start = ((), (), s32[]{:S(2)}) async-start(), calls=%async_computation.2 | async-start | bytes 3391488 | tf_op jit(solution)/shard_map/reduce_scatter | solution.py:153
  99.3 13.9 %copy-start.12 = (s32[8]{0:T(128)S(1)}, s32[8]{0:T(128)}, u32[]{:S(2)}) copy-start(s32[8]{0:T(128)} %param.22) | copy-start | bytes 100
  128.7 3.5 copy-start.2
  131.0 1.1 copy-start.1
  151.3 3.5 copy-start.2
  153.7 1.1 copy-start.1
  159.4 74.5 %copy-start.6 = (f32[976,128]{1,0:T(8,128)S(1)}, f32[976,128]{1,0:T(8,128)}, u32[]{:S(2)}) copy-start(f32[976,128]{1,0:T(8,128)} %copy-done.5) | copy-start | bytes 1499140
  159.4 74.8 %copy-start.4 = (bf16[976,768]{1,0:T(8,128)(2,1)S(1)}, bf16[976,768]{1,0:T(8,128)(2,1)}, u32[]{:S(2)}) copy-start(bf16[976,768]{1,0:T(8,128)(2,1)} %copy-done.3) | copy-start | bytes 4497412
  159.4 147.4 %all-reduce.3.cloned.1.call-start = ((), (), s32[]{:S(2)}) async-start(), calls=%async_computation.3 | async-start | bytes 786432 | tf_op jit(solution)/shard_map/psum | solution.py:99
  231.7 102.1 %copy-start.7 = (f32[4,180,128]{2,1,0:T(8,128)S(1)}, f32[4,180,128]{2,1,0:T(8,128)}, u32[]{:S(2)}) copy-start(f32[4,180,128]{2,1,0:T(8,128)} %reduce-scatter.2.cloned.1.call-done) | copy-start | bytes 1105924
  235.6 105.3 %all-reduce.5.cloned.1.call-start = ((), (), s32[]{:S(2)}) async-start(), calls=%async_computation.4 | async-start | bytes 786432 | tf_op jit(solution)/shard_map/psum | solution.py:99
Sparse Core Ops, SparseCore 0:
  52.9 46.3 all-gather.2
  159.6 72.0 reduce-scatter.1
  235.7 71.0 all-reduce.2
  309.0 31.8 all-reduce.4
